TPU v7x, 512 devices: a whole 4x4x16 slice. The times are simulated.
512 devices in a mesh: feat: 64 (over x, z), dom: 8 (over y, core).
Axes of the slice: x: 4, y: 4, z: 16, core: 2. Of those that a mesh axis runs over, the one named last changes fastest.
Arguments:
- features: bfloat16 [65536, 1024], P('dom', 'feat'), may hold values from -6 to 6
- self_weight: bfloat16 [1024, 512], P('feat'), may hold values from -0.1875 to 0.1875
- neighbour_weight: bfloat16 [1024, 512], P('feat'), may hold values from -1.5 to 1.5
- cotangent: bfloat16 [65536, 512], P(('dom', 'feat')), may hold values from -0.09375 to 0.09375
- send_rows: int32 [8, 8, 256], replicated, may hold values from 0 to 8191
- send_count: int32 [8, 8], replicated, may hold values from 32 to 256, as said below
- tile_source: int32 [8, 64, 8], P('dom'), may hold values from 0 to 79
- tile_kind: int32 [8, 64, 8], P('dom'), may hold values from 0 to 63
- tile_patterns: bfloat16 [64, 128, 128], replicated, may hold values from 0.0099487305 to 1
Outputs:
- hidden: bfloat16 [65536, 512], P(('dom', 'feat'))
- grad_self: float32 [1024, 512], P('feat')
- grad_neighbour: float32 [1024, 512], P('feat')
Inputs may be any that keep to these rules, and one draw needn't show every extreme that they name: `send_count`: one destination has 256 live slots from every owner.
All inputs are finite; a program needn't handle non-finite values.
Results may differ from a plain program's by a relative error of at most 0.005.
Values may be sent and summed in bfloat16 or wider, within the bound.
A program may use at most 128 MiB of HBM per device.

v0:
```python
import jax
import jax.numpy as jnp
from jax import lax
from jax.sharding import PartitionSpec as P

inv_root_two = 0.7071067811865476
inv_root_two_pi = 0.3989422804014327


def gelu_pair(linear):
    normal_cdf = 0.5 * (1.0 + jax.scipy.special.erf(linear * inv_root_two))
    density = jnp.exp(-0.5 * linear * linear) * inv_root_two_pi
    return (linear * normal_cdf, normal_cdf + linear * density)


def on_device(
    features,
    self_weight,
    neighbour_weight,
    cotangent,
    send_rows,
    send_count,
    tile_source,
    tile_kind,
    tile_patterns,
):
    my_part = lax.axis_index("dom")
    part_count = lax.axis_size("dom")
    row_count = features.shape[0]
    col_count = features.shape[1]
    slot_count = send_rows.shape[2]
    tile_rows = tile_patterns.shape[1]
    slot_ids = jnp.arange(slot_count, dtype=jnp.int32)
    everything = lax.all_gather(features, "dom", axis=0, tiled=True)
    wanted = lax.dynamic_index_in_dim(send_rows, my_part, 1, keepdims=False)
    counts = lax.dynamic_index_in_dim(send_count, my_part, 1, keepdims=False)
    flat_ids = jnp.arange(part_count, dtype=jnp.int32)[:, None] * row_count + wanted
    remote = everything[flat_ids.reshape(-1)].reshape(part_count, slot_count, col_count)
    live_mask = slot_ids[None, :] < counts[:, None]
    remote = jnp.where(live_mask[:, :, None], remote, jnp.zeros((), jnp.bfloat16))
    extended = jnp.concatenate([features, remote.reshape(-1, col_count)], 0).reshape(
        -1, tile_rows, col_count
    )
    kinds = tile_kind[0]
    tile_mats = tile_patterns[kinds]
    sources = extended[tile_source[0]]
    summed = jnp.einsum("tkab,tkbf->taf", tile_mats, sources, preferred_element_type=jnp.float32)
    pattern_sums = jnp.sum(tile_patterns, axis=2, dtype=jnp.float32)
    degree = jnp.sum(pattern_sums[kinds], axis=1)
    neighbour_mean = (
        (summed / degree[:, :, None]).reshape(row_count, col_count).astype(jnp.bfloat16)
    )
    own_features, own_mean = (
        lax.all_to_all(features, "feat", split_axis=0, concat_axis=1, tiled=True),
        lax.all_to_all(neighbour_mean, "feat", split_axis=0, concat_axis=1, tiled=True),
    )
    linear = jnp.dot(
        own_features,
        lax.all_gather(self_weight, "feat", axis=0, tiled=True),
        preferred_element_type=jnp.float32,
    ) + jnp.dot(
        own_mean,
        lax.all_gather(neighbour_weight, "feat", axis=0, tiled=True),
        preferred_element_type=jnp.float32,
    )
    gelu_value, gelu_slope = gelu_pair(linear)
    hidden = gelu_value.astype(jnp.bfloat16)
    grad_linear = (cotangent.astype(jnp.float32) * gelu_slope).astype(jnp.bfloat16)
    shard_rows = lax.all_gather(grad_linear, "feat", axis=0, tiled=True)
    self_part = jnp.einsum("rc,rh->ch", features, shard_rows, preferred_element_type=jnp.float32)
    neigh_part = jnp.einsum(
        "rc,rh->ch", neighbour_mean, shard_rows, preferred_element_type=jnp.float32
    )
    self_local, neigh_local = (self_part, neigh_part)
    grad_self, grad_neighbour = lax.psum((self_local, neigh_local), "dom")
    return (hidden, grad_self, grad_neighbour)


def solution(mesh):
    placed = (
        P("dom", "feat"),
        P("feat", None),
        P("feat", None),
        P(("dom", "feat"), None),
        P(),
        P(),
        P("dom", None, None),
        P("dom", None, None),
        P(),
    )
    return jax.shard_map(
        on_device,
        mesh=mesh,
        in_specs=placed,
        out_specs=(P(("dom", "feat"), None), P("feat", None), P("feat", None)),
        check_vma=False,
    )
```

profile of v0, /device:TPU:2, one launch (start us, length us, event | category | flops | bytes accessed | tf_op | source)
XLA Modules:
  0.0 632.6 jit_solution(4560406625717011600)
XLA Ops:
  7.2 0.0 copy-start
  7.2 0.0 copy-start.1
  7.2 0.0 all-gather.7.cloned.1.call-start
  7.2 2.7 copy.29
  10.0 0.0 all-gather.7.cloned.1.call-update
  10.0 0.0 all-gather.5.cloned.1.call-start
  10.1 0.7 all-gather.5.cloned.1.call-update
  10.8 1.7 copy_bitcast_fusion.1
  12.5 18.6 %all-to-all-start = ((bf16[64,128,16]{1,2,0:T(8,128)(2,1)}), bf16[64,128,16]{1,2,0:T(8,128)(2,1)S(1)}, u32[]{:S(2)}, u32[]{:S(2)}) async-start(bf16[64,128,16]{1,2,0:T(8,128)(2,1)} %copy_bitcast_fusion.1), calls=%async_computation | async-start | bytes 524288 | tf_op jit(solution)/shard_map/all_to_all | solution.py:54
  31.1 0.0 all-gather.9.cloned.1.call-start
  31.2 0.7 all-gather.9.cloned.1.call-update
  31.9 0.1 broadcast_bitcast_fusion
  32.0 0.9 dynamic-slice_reduce_fusion
  32.9 0.1 iota_compare_fusion
  33.0 0.7 compare_select_fusion.1
  33.7 0.1 copy.31
  33.8 0.1 reshape.150
  33.9 0.7 compare_select_fusion.2
  34.6 0.1 copy.28
  34.7 0.1 reshape.134
  34.8 2.5 convert_reduce_fusion
  37.3 14.0 %gather_fusion = bf16[512,128,128]{2,1,0:T(8,128)(2,1)} fusion(bf16[64,128,128]{2,1,0:T(8,128)(2,1)S(1)} %copy-done.1, s32[1024]{0:T(1024)S(1)} %pad_clamp_fusion.1), kind=kCustom, calls=%fused_computation | custom fusion | bytes 33556480 | tf_op jit(solution)/shard_map/gather | solution.py:45
  51.3 1.0 gather_fusion.3
  52.3 0.1 bitcast_reduce_fusion
  52.4 54.8 %all-gather.7.cloned.1.call-done = bf16[65536,16]{1,0:T(8,128)(2,1)} async-done(((bf16[8192,16]{1,0:T(8,128)(2,1)}), bf16[65536,16]{1,0:T(8,128)(2,1)}) %all-gather.7.cloned.1.call-update) | async-done | bytes 2097168 | tf_op jit(solution)/shard_map/all_gather | solution.py:34
  107.2 13.5 %gather_fusion.1 = bf16[2048,16]{1,0:T(8,128)(2,1)S(1)} fusion(bf16[65536,16]{1,0:T(8,128)(2,1)} %all-gather.7.cloned.1.call-done, s32[2048]{0:T(1024)S(1)} %broadcast_clamp_fusion), kind=kCustom, calls=%fused_computation.1 | custom fusion | bytes 139264 | tf_op jit(solution)/shard_map/gather | solution.py:38
  120.8 0.3 broadcast_select_fusion
  121.1 0.2 copy.30
  121.3 0.1 copy_bitcast_fusion
  121.4 2.0 gather_fusion.2
  123.4 0.0 copy-start.4
  123.4 8.9 %fusion.1 = bf16[64,128,16]{1,2,0:T(8,128)(2,1)} fusion(bf16[64,8,128,128]{3,2,1,0:T(8,128)(2,1)} %bitcast.61, bf16[64,8,128,16]{2,3,1,0:T(8,128)(2,1)S(1)} %bitcast.60, f32[64,128]{1,0:T(8,128)S(1)} %bitcast_reduce_fusion), kind=kOutput, calls=%fused_computation.9 | convolution fusion | flops 268697600 | bytes 19169280 | tf_op jit(solution)/shard_map/tkab,tkbf->taf/dot_general | solution.py:47
  132.3 15.7 %all-to-all-start.1 = ((bf16[64,128,16]{1,2,0:T(8,128)(2,1)}), bf16[64,128,16]{1,2,0:T(8,128)(2,1)S(1)}, u32[]{:S(2)}, u32[]{:S(2)}) async-start(bf16[64,128,16]{1,2,0:T(8,128)(2,1)} %fusion.1), calls=%async_computation.1 | async-start | bytes 524288 | tf_op jit(solution)/shard_map/all_to_all | solution.py:55
  148.0 0.0 all-gather.11.cloned.1.call-start
  148.0 102.2 %all-gather.5.cloned.1.call-done = bf16[1024,512]{1,0:T(8,128)(2,1)} async-done(((bf16[16,512]{1,0:T(8,128)(2,1)}), bf16[1024,512]{1,0:T(8,128)(2,1)}) %all-gather.5.cloned.1.call-update) | async-done | bytes 1048592 | tf_op jit(solution)/shard_map/all_gather | solution.py:59
  250.2 1.5 fusion.11
  251.8 137.4 %all-gather.9.cloned.1.call-done = bf16[1024,512]{1,0:T(8,128)(2,1)} async-done(((bf16[16,512]{1,0:T(8,128)(2,1)}), bf16[1024,512]{1,0:T(8,128)(2,1)}) %all-gather.9.cloned.1.call-update) | async-done | bytes 1048592 | tf_op jit(solution)/shard_map/all_gather | solution.py:63
  389.2 2.3 fusion.7
  391.5 0.0 all-gather.11.cloned.1.call-update
  391.5 0.0 all-reduce.3.cloned.1.call-start
  391.6 152.3 %all-gather.11.cloned.1.call-done = bf16[8192,512]{1,0:T(8,128)(2,1)} async-done(((bf16[128,512]{1,0:T(8,128)(2,1)}), bf16[8192,512]{1,0:T(8,128)(2,1)}) %all-gather.11.cloned.1.call-update) | async-done | bytes 8388624 | tf_op jit(solution)/shard_map/all_gather | solution.py:69
  543.9 5.4 fusion.8
  549.3 0.4 copy-done.2
  549.7 1.8 convolution_bitcast_fusion.1
  551.5 0.0 all-reduce.3.cloned.1.call-update
  551.6 71.8 %all-reduce.3.cloned.1.call-done = (f32[16,512]{1,0:T(8,128)}, f32[16,512]{1,0:T(8,128)}) async-done(((f32[16,512]{1,0:T(8,128)}, f32[16,512]{1,0:T(8,128)}), (f32[16,512]{1,0:T(8,128)}, f32[16,512]{1,0:T(8,128)})) %all-reduce.3.cloned.1.call-update) | async-done | bytes 65552 | tf_op jit(solution)/shard_map/psum | solution.py:75
  623.3 1.4 copy.47
  624.7 1.4 copy.48
  (16 shorter events, 0.1 us)
Async XLA Ops:
  7.2 24.8 %copy-start = (s32[8,8,256]{2,1,0:T(8,128)S(1)}, s32[8,8,256]{2,1,0:T(8,128)}, u32[]{:S(2)}) copy-start(s32[8,8,256]{2,1,0:T(8,128)} %param.13) | copy-start | bytes 196612
  7.2 30.1 %copy-start.1 = (bf16[64,128,128]{2,1,0:T(8,128)(2,1)S(1)}, bf16[64,128,128]{2,1,0:T(8,128)(2,1)}, u32[]{:S(2)}) copy-start(bf16[64,128,128]{2,1,0:T(8,128)(2,1)} %param.17) | copy-start | bytes 6291460
  7.2 100.0 %all-gather.7.cloned.1.call-start = ((), (), s32[]{:S(2)}) async-start(), calls=%async_computation.3 | async-start | bytes 18874368 | tf_op jit(solution)/shard_map/all_gather | solution.py:34
  10.0 240.2 %all-gather.5.cloned.1.call-start = ((), (), s32[]{:S(2)}) async-start(), calls=%async_computation.2 | async-start | bytes 1064960 | tf_op jit(solution)/shard_map/all_gather | solution.py:59
  12.5 119.8 %all-to-all-start = ((bf16[64,128,16]{1,2,0:T(8,128)(2,1)}), bf16[64,128,16]{1,2,0:T(8,128)(2,1)S(1)}, u32[]{:S(2)}, u32[]{:S(2)}) async-start(bf16[64,128,16]{1,2,0:T(8,128)(2,1)} %copy_bitcast_fusion.1), calls=%async_computation | async-start | bytes 524288 | tf_op jit(solution)/shard_map/all_to_all | solution.py:54
  31.1 358.1 %all-gather.9.cloned.1.call-start = ((), (), s32[]{:S(2)}) async-start(), calls=%async_computation.4 | async-start | bytes 1064960 | tf_op jit(solution)/shard_map/all_gather | solution.py:63
  51.3 70.0 %copy-start.3 = (bf16[8192,16]{0,1:T(8,128)(2,1)S(1)}, bf16[8192,16]{0,1:T(8,128)(2,1)}, u32[]{:S(2)}) copy-start(bf16[8192,16]{0,1:T(8,128)(2,1)} %param.9) | copy-start | bytes 786436
  123.4 265.8 %copy-start.4 = (bf16[128,512]{1,0:T(8,128)(2,1)S(1)}, bf16[128,512]{1,0:T(8,128)(2,1)}, u32[]{:S(2)}) copy-start(bf16[128,512]{1,0:T(8,128)(2,1)} %param.12) | copy-start | bytes 393220
  132.3 256.9 %all-to-all-start.1 = ((bf16[64,128,16]{1,2,0:T(8,128)(2,1)}), bf16[64,128,16]{1,2,0:T(8,128)(2,1)S(1)}, u32[]{:S(2)}, u32[]{:S(2)}) async-start(bf16[64,128,16]{1,2,0:T(8,128)(2,1)} %fusion.1), calls=%async_computation.1 | async-start | bytes 524288 | tf_op jit(solution)/shard_map/all_to_all | solution.py:55
  148.0 395.9 %all-gather.11.cloned.1.call-start = ((), (), s32[]{:S(2)}) async-start(), calls=%async_computation.5 | async-start | bytes 8519680 | tf_op jit(solution)/shard_map/all_gather | solution.py:69
  391.5 231.8 %all-reduce.3.cloned.1.call-start = ((), (), s32[]{:S(2)}) async-start(), calls=%async_computation.6 | async-start | bytes 131072 | tf_op jit(solution)/shard_map/psum | solution.py:75
  543.9 5.9 copy-start.2
Sparse Core Ops, SparseCore 0:
  10.2 97.0 all-gather.6
  110.2 140.0 all-gather.4
  253.2 135.9 all-gather.8
  392.0 151.8 all-gather.10
  551.7 71.6 all-reduce.2
where the time goes:
time: 633 us
  waiting for transfers between devices  520 us (82%)
  local copies, waits for them, and re-layouts  39.7 us (6%)
  starting transfers between devices  34.6 us (5%)
  matrix products  20 us (3%)
  between operations  13.9 us (2%)
    all_gather x1, waiting for transfers between devices, on_device(): shard_rows = lax.all_gather(grad_linear, 'feat', axis=0, tiled=True)  152 us
    all_gather x1, waiting for transfers between devices, on_device(): lax.all_gather(neighbour_weight, 'feat', axis=0, tiled=True)  137 us
    all_gather x1, waiting for transfers between devices, on_device(): lax.all_gather(self_weight, 'feat', axis=0, tiled=True)  102 us
    psum x1, waiting for transfers between devices, on_device(): grad_self, grad_neighbour = lax.psum((self_local, neigh_local), 'dom')  71.8 us
    all_gather x1, waiting for transfers between devices, on_device(): everything = lax.all_gather(features, 'dom', axis=0, tiled=True)  54.8 us
    all_to_all x1, starting transfers between devices, on_device(): lax.all_to_all(features, 'feat', split_axis=0, concat_axis=1, tiled=True)  18.6 us
    all_to_all x1, starting transfers between devices, on_device(): lax.all_to_all(neighbour_mean, 'feat', split_axis=0, concat_axis=1, tiled...  15.7 us
    gather x1, local copies, waits for them, and re-layouts, on_device(): tile_mats = tile_patterns[kinds]  14 us
  transfers between devices with their start and end apart: 7, of which 5 were waited for; matrix products, arithmetic and copies ran while one was open for 8% of the time, Pallas kernels for 0%

commit v1 on v0

--- a/solution.py
+++ b/solution.py
@@ -66,7 +66,9 @@
     gelu_value, gelu_slope = gelu_pair(linear)
     hidden = gelu_value.astype(jnp.bfloat16)
     grad_linear = (cotangent.astype(jnp.float32) * gelu_slope).astype(jnp.bfloat16)
-    shard_rows = lax.all_gather(grad_linear, "feat", axis=0, tiled=True)
+    shard_rows = jnp.concatenate(
+        lax.all_to_all(jnp.stack([grad_linear] * lax.axis_size("feat")), "feat", 0, 0), axis=0
+    )
     self_part = jnp.einsum("rc,rh->ch", features, shard_rows, preferred_element_type=jnp.float32)
     neigh_part = jnp.einsum(
         "rc,rh->ch", neighbour_mean, shard_rows, preferred_element_type=jnp.float32

time: 633 us -> 844 us (1.33)
  blocking collectives: 0 us -> 365 us
  waiting for transfers between devices: 520 us -> 367 us
    all_to_all x0 -> x1, blocking collectives: none -> 365 us  [on_device(): lax.all_to_all(jnp.stack([grad_linear] * lax.axis_size('feat')), 'feat',...]
    all_gather x1 -> x0, waiting for transfers between devices: 152 us -> none  [on_device(): shard_rows = lax.all_gather(grad_linear, 'feat', axis=0, tiled=True)]
  transfers between devices with their start and end apart: 7 -> 6, of which waited for: 5 -> 4; matrix products, arithmetic and copies ran while one was open for 8% -> 6% of each run, Pallas kernels for 0% -> 0%
where the time goes in v1:
time: 844 us; the launch traced here: 843 us
  waiting for transfers between devices  367 us (43%)
  blocking collectives  365 us (43%)
  local copies, waits for them, and re-layouts  40.3 us (5%)
  starting transfers between devices  34.7 us (4%)
  matrix products  17.3 us (2%)
  between operations  13.9 us (2%)
    all_to_all x1, blocking collectives, on_device(): lax.all_to_all(jnp.stack([grad_linear] * lax.axis_size('feat')), 'feat',...  365 us
    all_gather x1, waiting for transfers between devices, on_device(): lax.all_gather(neighbour_weight, 'feat', axis=0, tiled=True)  137 us
    all_gather x1, waiting for transfers between devices, on_device(): lax.all_gather(self_weight, 'feat', axis=0, tiled=True)  102 us
    psum x1, waiting for transfers between devices, on_device(): grad_self, grad_neighbour = lax.psum((self_local, neigh_local), 'dom')  71.3 us
    all_gather x1, waiting for transfers between devices, on_device(): everything = lax.all_gather(features, 'dom', axis=0, tiled=True)  54.7 us
    all_to_all x1, starting transfers between devices, on_device(): lax.all_to_all(features, 'feat', split_axis=0, concat_axis=1, tiled=True)  18.6 us
  transfers between devices with their start and end apart: 6, of which 4 were waited for; matrix products, arithmetic and copies ran while one was open for 6% of the time, Pallas kernels for 0%

profile of v1, /device:TPU:2, one launch (start us, length us, event | category | flops | bytes accessed | tf_op | source)
XLA Modules:
  0.0 843.1 jit_solution(14438376030110432339)
XLA Ops:
  7.2 0.0 copy-start
  7.2 0.0 copy-start.1
  7.2 0.0 all-gather.6.cloned.1.call-start
  7.2 2.8 copy.27
  10.0 0.0 all-gather.6.cloned.1.call-update
  10.0 0.0 all-gather.4.cloned.1.call-start
  10.1 0.7 all-gather.4.cloned.1.call-update
  10.8 1.7 copy_bitcast_fusion.1
  12.5 18.6 %all-to-all-start = ((bf16[64,128,16]{1,2,0:T(8,128)(2,1)}), bf16[64,128,16]{1,2,0:T(8,128)(2,1)S(1)}, u32[]{:S(2)}, u32[]{:S(2)}) async-start(bf16[64,128,16]{1,2,0:T(8,128)(2,1)} %copy_bitcast_fusion.1), calls=%async_computation | async-start | bytes 524288 | tf_op jit(solution)/shard_map/all_to_all | solution.py:54
  31.1 0.0 all-gather.8.cloned.1.call-start
  31.2 0.7 all-gather.8.cloned.1.call-update
  31.9 0.1 broadcast_bitcast_fusion
  32.0 0.9 dynamic-slice_reduce_fusion
  32.9 0.1 iota_compare_fusion
  33.0 0.7 compare_select_fusion.1
  33.7 0.1 copy.29
  33.8 0.1 reshape.156
  33.9 0.7 compare_select_fusion.2
  34.6 0.1 copy.26
  34.7 0.1 reshape.140
  34.8 2.6 convert_reduce_fusion
  37.4 14.0 %gather_fusion = bf16[512,128,128]{2,1,0:T(8,128)(2,1)} fusion(bf16[64,128,128]{2,1,0:T(8,128)(2,1)S(1)} %copy-done.1, s32[1024]{0:T(1024)S(1)} %pad_clamp_fusion.1), kind=kCustom, calls=%fused_computation | custom fusion | bytes 33556480 | tf_op jit(solution)/shard_map/gather | solution.py:45
  51.4 1.0 gather_fusion.3
  52.4 0.1 bitcast_reduce_fusion
  52.5 54.7 %all-gather.6.cloned.1.call-done = bf16[65536,16]{1,0:T(8,128)(2,1)} async-done(((bf16[8192,16]{1,0:T(8,128)(2,1)}), bf16[65536,16]{1,0:T(8,128)(2,1)}) %all-gather.6.cloned.1.call-update) | async-done | bytes 2097168 | tf_op jit(solution)/shard_map/all_gather | solution.py:34
  107.2 13.5 %gather_fusion.1 = bf16[2048,16]{1,0:T(8,128)(2,1)S(1)} fusion(bf16[65536,16]{1,0:T(8,128)(2,1)} %all-gather.6.cloned.1.call-done, s32[2048]{0:T(1024)S(1)} %broadcast_clamp_fusion), kind=kCustom, calls=%fused_computation.1 | custom fusion | bytes 139264 | tf_op jit(solution)/shard_map/gather | solution.py:38
  120.8 0.3 broadcast_select_fusion
  121.1 0.2 copy.28
  121.3 0.1 copy_bitcast_fusion
  121.4 2.0 gather_fusion.2
  123.4 0.0 copy-start.3
  123.4 8.9 %fusion.1 = bf16[64,128,16]{1,2,0:T(8,128)(2,1)} fusion(bf16[64,8,128,128]{3,2,1,0:T(8,128)(2,1)} %bitcast.59, bf16[64,8,128,16]{2,3,1,0:T(8,128)(2,1)S(1)} %bitcast.58, f32[64,128]{1,0:T(8,128)S(1)} %bitcast_reduce_fusion), kind=kOutput, calls=%fused_computation.10 | convolution fusion | flops 268697600 | bytes 19169280 | tf_op jit(solution)/shard_map/tkab,tkbf->taf/dot_general | solution.py:47
  132.3 0.0 all-to-all-done
  132.3 15.7 %all-to-all-start.1 = ((bf16[64,128,16]{1,2,0:T(8,128)(2,1)}), bf16[64,128,16]{1,2,0:T(8,128)(2,1)S(1)}, u32[]{:S(2)}, u32[]{:S(2)}) async-start(bf16[64,128,16]{1,2,0:T(8,128)(2,1)} %fusion.1), calls=%async_computation.1 | async-start | bytes 524288 | tf_op jit(solution)/shard_map/all_to_all | solution.py:55
  148.0 0.2 all-reduce.3.cloned.1.call-start
  148.2 102.0 %all-gather.4.cloned.1.call-done = bf16[1024,512]{1,0:T(8,128)(2,1)} async-done(((bf16[16,512]{1,0:T(8,128)(2,1)}), bf16[1024,512]{1,0:T(8,128)(2,1)}) %all-gather.4.cloned.1.call-update) | async-done | bytes 1048592 | tf_op jit(solution)/shard_map/all_gather | solution.py:59
  250.2 1.5 fusion.8
  251.8 137.4 %all-gather.8.cloned.1.call-done = bf16[1024,512]{1,0:T(8,128)(2,1)} async-done(((bf16[16,512]{1,0:T(8,128)(2,1)}), bf16[1024,512]{1,0:T(8,128)(2,1)}) %all-gather.8.cloned.1.call-update) | async-done | bytes 1048592 | tf_op jit(solution)/shard_map/all_gather | solution.py:63
  389.2 0.0 all-to-all-done.1
  389.2 2.3 fusion.7
  391.5 1.0 stack.2
  392.5 365.5 %all_to_all.40 = bf16[64,128,512]{2,1,0:T(8,128)(2,1)S(1)} all-to-all(bf16[64,128,512]{2,1,0:T(8,128)(2,1)S(1)} %stack.2), channel_id=1, replica_groups=mesh['feat'=64,'dom'=8] {'feat'}, dimensions={0} | all-to-all | bytes 16777216 | tf_op jit(solution)/shard_map/all_to_all | solution.py:70
  757.9 1.8 convolution_bitcast_fusion.1
  759.8 2.8 convolution_bitcast_fusion.2
  762.5 0.0 all-reduce.3.cloned.1.call-update
  762.5 71.3 %all-reduce.3.cloned.1.call-done = (f32[16,512]{1,0:T(8,128)}, f32[16,512]{1,0:T(8,128)}) async-done(((f32[16,512]{1,0:T(8,128)}, f32[16,512]{1,0:T(8,128)}), (f32[16,512]{1,0:T(8,128)}, f32[16,512]{1,0:T(8,128)})) %all-reduce.3.cloned.1.call-update) | async-done | bytes 65552 | tf_op jit(solution)/shard_map/psum | solution.py:77
  833.8 1.4 copy.39
  835.2 1.4 copy.40
  (13 shorter events, 0.1 us)
Async XLA Ops:
  7.2 24.8 %copy-start = (s32[8,8,256]{2,1,0:T(8,128)S(1)}, s32[8,8,256]{2,1,0:T(8,128)}, u32[]{:S(2)}) copy-start(s32[8,8,256]{2,1,0:T(8,128)} %param.13) | copy-start | bytes 196612
  7.2 30.2 %copy-start.1 = (bf16[64,128,128]{2,1,0:T(8,128)(2,1)S(1)}, bf16[64,128,128]{2,1,0:T(8,128)(2,1)}, u32[]{:S(2)}) copy-start(bf16[64,128,128]{2,1,0:T(8,128)(2,1)} %param.17) | copy-start | bytes 6291460
  7.2 100.0 %all-gather.6.cloned.1.call-start = ((), (), s32[]{:S(2)}) async-start(), calls=%async_computation.4 | async-start | bytes 18874368 | tf_op jit(solution)/shard_map/all_gather | solution.py:34
  10.0 240.2 %all-gather.4.cloned.1.call-start = ((), (), s32[]{:S(2)}) async-start(), calls=%async_computation.3 | async-start | bytes 1064960 | tf_op jit(solution)/shard_map/all_gather | solution.py:59
  12.5 119.8 %all-to-all-start = ((bf16[64,128,16]{1,2,0:T(8,128)(2,1)}), bf16[64,128,16]{1,2,0:T(8,128)(2,1)S(1)}, u32[]{:S(2)}, u32[]{:S(2)}) async-start(bf16[64,128,16]{1,2,0:T(8,128)(2,1)} %copy_bitcast_fusion.1), calls=%async_computation | async-start | bytes 524288 | tf_op jit(solution)/shard_map/all_to_all | solution.py:54
  31.1 358.0 %all-gather.8.cloned.1.call-start = ((), (), s32[]{:S(2)}) async-start(), calls=%async_computation.5 | async-start | bytes 1064960 | tf_op jit(solution)/shard_map/all_gather | solution.py:63
  51.4 69.9 %copy-start.2 = (bf16[8192,16]{0,1:T(8,128)(2,1)S(1)}, bf16[8192,16]{0,1:T(8,128)(2,1)}, u32[]{:S(2)}) copy-start(bf16[8192,16]{0,1:T(8,128)(2,1)} %param.9) | copy-start | bytes 786436
  123.4 265.8 %copy-start.3 = (bf16[128,512]{1,0:T(8,128)(2,1)S(1)}, bf16[128,512]{1,0:T(8,128)(2,1)}, u32[]{:S(2)}) copy-start(bf16[128,512]{1,0:T(8,128)(2,1)} %param.12) | copy-start | bytes 393220
  132.3 256.9 %all-to-all-start.1 = ((bf16[64,128,16]{1,2,0:T(8,128)(2,1)}), bf16[64,128,16]{1,2,0:T(8,128)(2,1)S(1)}, u32[]{:S(2)}, u32[]{:S(2)}) async-start(bf16[64,128,16]{1,2,0:T(8,128)(2,1)} %fusion.1), calls=%async_computation.1 | async-start | bytes 524288 | tf_op jit(solution)/shard_map/all_to_all | solution.py:55
  148.0 685.8 %all-reduce.3.cloned.1.call-start = ((), (), s32[]{:S(2)}) async-start(), calls=%async_computation.6 | async-start | bytes 131072 | tf_op jit(solution)/shard_map/psum | solution.py:77
Sparse Core Ops, SparseCore 0:
  10.2 97.0 all-gather.5
  110.2 140.0 all-gather.3
  253.2 135.9 all-gather.7
  762.7 71.1 all-reduce.2
